TPU v7x, 32 devices: a whole 2x2x4 slice. The times are simulated.
32 devices in a mesh: row: 4 (over y, core), col: 8 (over z, x).
Axes of the slice: x: 2, y: 2, z: 4, core: 2. Of those that a mesh axis runs over, the one named last changes fastest.
Arguments:
- states_now: float32 [40, 4096], P(None, ('col', 'row')), may hold values from -60 to 60
- states_next: float32 [40, 4096], P(None, ('row', 'col')), may hold values from -60 to 60
- states_last: float32 [40, 4096], P(None, ('col', 'row')), may hold values from -60 to 60
- payoff_now: bfloat16 [64, 4096], P(None, ('col', 'row')), may hold values from 0 to 2
- payoff_next: bfloat16 [64, 4096], P(None, ('row', 'col')), may hold values from 0 to 2
- payoff_last: bfloat16 [64, 4096], P(None, ('col', 'row')), may hold values from 0 to 2
Outputs:
- value_next: float32 [64, 4096], P(None, ('row', 'col'))
- value_now: float32 [64, 4096], P(None, ('col', 'row'))
All inputs are finite; a program needn't handle non-finite values.
Results may differ from a plain program's by a relative error of at most 0.0003.
Values sent between devices are 32-bit elements; how exact they have to be, the bound alone decides.
No kernel may reach another device: no remote copies, remote signals or barrier semaphores. Data moves between devices by JAX's collectives and lax.ppermute only.
A program may use at most 128 MiB of HBM per device.

v0:
```python
import math

import jax
import jax.numpy as jnp
from jax import lax
from jax.sharding import PartitionSpec as P


def merged(array, axis, combine):
    everything = jax.tree.map(lambda part: lax.all_gather(part, axis), array)
    first = jax.tree.map(lambda part: part[0], everything)

    def lap(k, so_far):
        return combine(so_far, jax.tree.map(lambda part: part[k], everything))

    return lax.fori_loop(1, lax.axis_size(axis), lap, first)


def log_kernel(row_states, col_states, row_norms, col_norms):
    cross_term = lax.dot_general(
        row_states,
        col_states,
        (((0,), (0,)), ((), ())),
        precision=lax.Precision.HIGHEST,
        preferred_element_type=jnp.float32,
    )
    return cross_term - 0.5 * row_norms[:, None] - 0.5 * col_norms[None, :]


def log_blocks(row_states, col_states):
    factors, points = row_states.shape
    block_rows = math.gcd(points, 512)
    block_count = points // block_rows
    blocks = row_states.reshape(factors, block_count, block_rows).transpose(1, 0, 2)
    norms = jnp.sum(row_states * row_states, axis=0).reshape(block_count, block_rows)
    col_norms = jnp.sum(col_states * col_states, axis=0)

    def build(block_item):
        row_piece, piece_norms = block_item
        return log_kernel(row_piece, col_states, piece_norms, col_norms)

    return lax.map(build, (blocks, norms))


def local_stats(log_weight):
    col_peak = jnp.max(log_weight, axis=(0, 1))
    col_sum = jnp.sum(jnp.exp(log_weight - col_peak[None, None, :]), axis=(0, 1))
    return (col_peak, col_sum)


def join_stats(earlier_pair, later_pair):
    new_peak = jnp.maximum(earlier_pair[0], later_pair[0])
    joined = earlier_pair[1] * jnp.exp(earlier_pair[0] - new_peak) + later_pair[1] * jnp.exp(
        later_pair[0] - new_peak
    )
    return (new_peak, joined)


def stats_row(col_peak, col_sum):
    global_peak = lax.pmax(col_peak, "row")
    global_sum = lax.psum(col_sum * jnp.exp(col_peak - global_peak), "row")
    return (global_peak, global_sum)


def stats_col(col_peak, col_sum):
    return merged((col_peak, col_sum), "col", join_stats)


def continuation(log_weight, later_value, col_peak, col_sum):
    scaled = (later_value / col_sum[None, :]).astype(jnp.bfloat16)

    def project(weight_block):
        kernel = jnp.exp(weight_block - col_peak[None, :]).astype(jnp.bfloat16)
        return lax.dot_general(
            scaled, kernel, (((1,), (1,)), ((), ())), preferred_element_type=jnp.float32
        )

    pieces = lax.map(project, log_weight)
    block_count, block_rows = (log_weight.shape[0], log_weight.shape[1])
    return pieces.transpose(1, 0, 2).reshape(scaled.shape[0], block_count * block_rows)


def per_device(states_now, states_next, states_last, payoff_now, payoff_next, payoff_last):
    own_points = payoff_next.shape[1]
    later_states, later_values = (
        lax.all_gather(states_last, "row", axis=1, tiled=True),
        lax.all_gather(payoff_last.astype(jnp.float32), "row", axis=1, tiled=True),
    )
    next_rows, next_payoff = (
        lax.all_gather(states_next, "col", axis=1, tiled=True),
        lax.all_gather(payoff_next.astype(jnp.float32), "col", axis=1, tiled=True),
    )
    weights = log_blocks(next_rows, later_states)
    col_peak, col_sum = local_stats(weights)
    col_peak, col_sum = stats_row(col_peak, col_sum)
    partial_value = continuation(weights, later_values, col_peak, col_sum)
    whole_sum = lax.psum(partial_value, "col")
    value_block = jnp.maximum(next_payoff, whole_sum)
    value_next = lax.dynamic_slice_in_dim(
        value_block, lax.axis_index("col") * own_points, own_points, 1
    )
    now_rows = lax.all_gather(states_now, "row", axis=1, tiled=True)
    weights = log_blocks(now_rows, next_rows)
    col_peak, col_sum = local_stats(weights)
    col_peak, col_sum = stats_col(col_peak, col_sum)
    partial_value = continuation(weights, value_block, col_peak, col_sum)
    own_block = lax.psum_scatter(partial_value, "row", scatter_dimension=1, tiled=True)
    value_now = jnp.maximum(payoff_now.astype(jnp.float32), own_block)
    return (value_next, value_now)


def solution(mesh):
    in_specs = (
        P(None, ("col", "row")),
        P(None, ("row", "col")),
        P(None, ("col", "row")),
        P(None, ("col", "row")),
        P(None, ("row", "col")),
        P(None, ("col", "row")),
    )
    out_specs = (P(None, ("row", "col")), P(None, ("col", "row")))
    return jax.shard_map(
        per_device, mesh=mesh, in_specs=in_specs, out_specs=out_specs, check_vma=False
    )
```

profile of v0, /device:TPU:0, one launch (start us, length us, event | category | flops | bytes accessed | tf_op | source)
XLA Modules:
  0.0 198.5 jit_solution(9412907396690079252)
XLA Ops:
  7.2 0.0 all-reduce.2.cloned.1.call-start
  7.2 32.6 %all_gather.28 = f32[40,1024]{1,0:T(8,128)S(1)} all-gather(f32[40,128]{1,0:T(8,128)} %param.13), channel_id=1, replica_groups=mesh['row'=4,'col'=8] {'col'}, dimensions={1}, use_global_device_ids=true | all-gather | bytes 184320 | tf_op jit(solution)/shard_map/all_gather | solution.py:90
  39.8 0.1 reshape.54
  40.0 5.5 %all_gather.29 = f32[40,512]{1,0:T(8,128)S(1)} all-gather(f32[40,128]{1,0:T(8,128)} %param.14), channel_id=1, replica_groups=mesh['row'=4,'col'=8] {'row'}, dimensions={1}, use_global_device_ids=true | all-gather | bytes 102400 | tf_op jit(solution)/shard_map/all_gather | solution.py:86
  45.5 2.4 %while.45 = (s32[]{:T(128)}, f32[2,512,512]{2,1,0:T(8,128)S(1)}, f32[2,40,512]{2,0,1:T(2,128)S(1)}, f32[40,512]{1,0:T(8,128)S(1)}, f32[2,512]{1,0:T(2,128)S(1)}, /*index=5*/f32[512]{0:T(512)S(1)}, s32[]{:T(128)}) while((s32[]{:T(128)}, f32[2,512,512]{2,1,0:T(8,128)S(1)}, f32[2,40,512]{2,0,1:T(2,128)S(1)}, f32[40,512]{1,0:T(8,128)S(1)}, ...), condition=%wide.region_3.4_spmd, body=%wide.region_2.3_spmd.sunk | while | flops 126354432 | bytes 1388633 | solution.py:42
  45.5 0.1 constant_dynamic-slice_fusion.6
  45.6 1.1 fusion.23
  46.7 0.1 constant_dynamic-slice_fusion.6
  46.8 1.1 fusion.23
  47.9 0.0 copy-start.1
  47.9 0.2 reduce_max.18
  48.1 0.4 exponential_reduce_fusion.1
  48.5 7.1 %pmax.7 = f32[512]{0:T(512)S(1)} all-reduce(f32[512]{0:T(512)S(1)} %reduce_max.18), channel_id=1, replica_groups=mesh['row'=4,'col'=8] {'row'}, use_global_device_ids=true, to_apply=%region_5.6 | all-reduce | flops 512 | bytes 4096 | tf_op jit(solution)/shard_map/pmax | solution.py:60
  55.6 5.9 %psum.14 = f32[512]{0:T(512)S(1)} all-reduce(f32[512]{0:T(512)S(1)} %exponential_multiply_fusion), channel_id=1, replica_groups=mesh['row'=4,'col'=8] {'row'}, use_global_device_ids=true, to_apply=%region_7.8 | all-reduce | flops 512 | bytes 4096 | tf_op jit(solution)/shard_map/psum | solution.py:61
  61.5 0.0 copy-done.1
  61.5 5.4 %all_gather.30 = f32[64,512]{1,0:T(8,128)S(1)} all-gather(f32[64,128]{1,0:T(8,128)S(1)} %convert_element_type.23), channel_id=1, replica_groups=mesh['row'=4,'col'=8] {'row'}, dimensions={1}, use_global_device_ids=true | all-gather | bytes 163840 | tf_op jit(solution)/shard_map/all_gather | solution.py:87
  66.9 0.0 copy-start
  66.9 0.6 while.46
  66.9 0.3 fusion.26
  67.3 0.3 fusion.26
  67.6 0.7 copy.14
  68.3 0.0 all-reduce.2.cloned.1.call-update
  68.3 0.0 reduce-scatter.2.cloned.1.call-start
  68.4 0.0 copy-done
  68.4 5.3 %all_gather.31 = f32[40,512]{1,0:T(8,128)S(1)} all-gather(f32[40,128]{1,0:T(8,128)S(1)} %copy-done), channel_id=1, replica_groups=mesh['row'=4,'col'=8] {'row'}, dimensions={1}, use_global_device_ids=true | all-gather | bytes 102400 | tf_op jit(solution)/shard_map/all_gather | solution.py:102
  73.7 0.0 copy-start.2
  73.7 2.0 fusion.12
  75.7 0.3 exponential_reduce_fusion
  76.0 30.6 %all-gather.1 = f32[8192]{0:T(1024)S(1)} all-gather(f32[1024]{0:T(1024)S(1)} %exponential_reduce_fusion), channel_id=3, replica_groups=mesh['row'=4,'col'=8] {'col'}, dimensions={0}, use_global_device_ids=true | all-gather | bytes 36864 | tf_op jit(solution)/shard_map/all_gather | solution.py:10
  106.6 30.7 %all-gather = f32[8192]{0:T(1024)S(1)} all-gather(f32[1024]{0:T(1024)S(1)} %get-tuple-element.279), channel_id=2, replica_groups=mesh['row'=4,'col'=8] {'col'}, dimensions={0}, use_global_device_ids=true | all-gather | bytes 36864 | tf_op jit(solution)/shard_map/all_gather | solution.py:10
  137.4 0.0 copy-start.3
  137.4 0.4 while.47
  137.8 0.0 copy-done.2
  137.8 30.7 %all_gather.27 = f32[64,1024]{1,0:T(8,128)S(1)} all-gather(f32[64,128]{1,0:T(8,128)S(1)} %convert_element_type.22), channel_id=1, replica_groups=mesh['row'=4,'col'=8] {'col'}, dimensions={1}, use_global_device_ids=true | all-gather | bytes 294912 | tf_op jit(solution)/shard_map/all_gather | solution.py:91
  168.6 0.0 all-reduce.2.cloned.1.call-done
  168.6 1.0 max.18
  169.6 1.1 fusion.9
  170.6 0.0 reduce-scatter.2.cloned.1.call-update
  170.7 0.6 constant_dynamic-slice_fusion.3
  171.3 19.0 %reduce-scatter.2.cloned.1.call-done = f32[64,128]{1,0:T(8,128)} async-done(((f32[64,512]{1,0:T(8,128)}), f32[64,128]{1,0:T(8,128)}) %reduce-scatter.2.cloned.1.call-update) | async-done | bytes 32784 | tf_op jit(solution)/shard_map/reduce_scatter | solution.py:107
  190.3 0.0 copy-done.3
  190.3 1.4 convert_maximum_fusion
  (34 shorter events, 0.4 us)
Async XLA Ops:
  7.2 161.4 %all-reduce.2.cloned.1.call-start = ((), (), s32[]{:S(2)}) async-start(), calls=%async_computation.1 | async-start | bytes 524288 | tf_op jit(solution)/shard_map/psum | solution.py:97
  47.9 13.6 %copy-start.1 = (bf16[64,128]{1,0:T(8,128)(2,1)S(1)}, bf16[64,128]{1,0:T(8,128)(2,1)}, u32[]{:S(2)}) copy-start(bf16[64,128]{1,0:T(8,128)(2,1)} %param.17) | copy-start | bytes 49156
  66.9 1.5 copy-start
  68.3 122.0 %reduce-scatter.2.cloned.1.call-start = ((), (), s32[]{:S(2)}) async-start(), calls=%async_computation.2 | async-start | bytes 163840 | tf_op jit(solution)/shard_map/reduce_scatter | solution.py:107
  73.7 64.1 %copy-start.2 = (bf16[64,128]{1,0:T(8,128)(2,1)S(1)}, bf16[64,128]{1,0:T(8,128)(2,1)}, u32[]{:S(2)}) copy-start(bf16[64,128]{1,0:T(8,128)(2,1)} %param.16) | copy-start | bytes 49156
  137.4 52.9 %copy-start.3 = (bf16[64,128]{1,0:T(8,128)(2,1)S(1)}, bf16[64,128]{1,0:T(8,128)(2,1)}, u32[]{:S(2)}) copy-start(bf16[64,128]{1,0:T(8,128)(2,1)} %param.15) | copy-start | bytes 49156
Sparse Core Ops, SparseCore 0:
  68.4 71.0 all-reduce.1
  170.8 19.4 reduce-scatter.1
where the time goes:
time: 199 us
  blocking collectives  154 us (77%)
  waiting for transfers between devices  19 us (10%)
  between operations  14.2 us (7%)
  matrix products  5.77 us (3%)
  other arithmetic  3.48 us (2%)
    all_gather x2, blocking collectives, merged(): everything = jax.tree.map(lambda part: lax.all_gather(part, axis), array)  61.3 us
    all_gather x1, blocking collectives, per_device(): lax.all_gather(states_next, 'col', axis=1, tiled=True)  32.6 us
    all_gather x1, blocking collectives, per_device(): lax.all_gather(payoff_next.astype(jnp.float32), 'col', axis=1, tiled=True)  30.7 us
    reduce_scatter x1, waiting for transfers between devices, per_device(): lax.psum_scatter(partial_value, 'row', scatter_dimension=1, tiled=True)  19 us
    pmax x1, blocking collectives, stats_row(): global_peak = lax.pmax(col_peak, 'row')  7.11 us
    psum x1, blocking collectives, stats_row(): global_sum = lax.psum(col_sum * jnp.exp(col_peak - global_peak), 'row')  5.88 us
    all_gather x1, blocking collectives, per_device(): lax.all_gather(states_last, 'row', axis=1, tiled=True)  5.49 us
    all_gather x1, blocking collectives, per_device(): lax.all_gather(payoff_last.astype(jnp.float32), 'row', axis=1, tiled=True)  5.42 us
  transfers between devices with their start and end apart: 2, of which 1 were waited for; matrix products, arithmetic and copies ran while one was open for 2% of the time, Pallas kernels for 0%

commit v1 on v0

v1 whole, which is shorter than its diff:
```python
import functools

import jax
import jax.numpy as jnp
from jax import lax
from jax.experimental import pallas as pl
from jax.experimental.pallas import tpu as pltpu
from jax.sharding import PartitionSpec as P

LANES = 128
SPLIT_ROWS = 8


def swapped(array, link):
    axis, bit = link
    pairs = [(i, i ^ bit) for i in range(lax.axis_size(axis))]
    return lax.ppermute(array, axis, pairs)


def bits(axis, lowest, end):
    size = lax.axis_size(axis)
    return [(axis, 1 << k) for k in range(lowest, size.bit_length() - 1) if (1 << k) < end]


def gathered(block, links):
    for link in links:
        block = jnp.concatenate([block, swapped(block, link)], axis=0)
    return block


def flipped(array, level):
    count = array.shape[0]
    step = 1 << level
    shape = (count // (2 * step), 2, step) + array.shape[1:]
    return jnp.flip(array.reshape(shape), axis=1).reshape(array.shape)


def summed(array, links):
    for level, link in enumerate(links):
        array = array + flipped(swapped(array, link), level)
    return array


def scattered(array, links):
    for link in reversed(links):
        half = array.shape[0] // 2
        array = array[:half] + swapped(array[half:], link)
    return array


def joined_stats(stats, links):
    for level, link in reversed(list(enumerate(links))):
        other = flipped(swapped(stats, link), level)
        peak = jnp.maximum(stats[:, :1], other[:, :1])
        total = stats[:, 1:] * jnp.exp(stats[:, :1] - peak) + other[:, 1:] * jnp.exp(other[:, :1] - peak)
        stats = jnp.concatenate([peak, total], axis=1)
    return stats


def thirds(x):
    high = x.astype(jnp.bfloat16).astype(jnp.float32)
    rest = x - high
    middle = rest.astype(jnp.bfloat16).astype(jnp.float32)
    return high, middle, rest - middle


def operand(states, earlier):
    high, middle, low = thirds(states)
    norm = thirds(-0.5 * jnp.sum(states * states, axis=0, keepdims=True))
    lanes = states.shape[1]
    row = lax.broadcasted_iota(jnp.int32, (SPLIT_ROWS, lanes), 0)
    first = 0 if earlier else 3
    tail = jnp.where(row < 6, 1.0, 0.0)
    for k in range(3):
        tail = jnp.where(row == first + k, norm[k], tail)
    if earlier:
        parts = [high, high, middle, middle, high, low, tail]
    else:
        parts = [high, middle, high, middle, low, high, tail]
    return jnp.concatenate(parts, axis=0).astype(jnp.bfloat16)


def weights_kernel(earlier_ref, later_ref, weight_ref, stats_ref):
    rows = jnp.concatenate([operand(earlier_ref[b], True) for b in range(earlier_ref.shape[0])], axis=1)
    width = weight_ref.shape[2]
    per = width // LANES
    for c in range(weight_ref.shape[0]):
        cols = jnp.concatenate([operand(later_ref[c * per + b], False) for b in range(per)], axis=1)
        log_weight = lax.dot_general(rows, cols, (((0,), (0,)), ((), ())), preferred_element_type=jnp.float32)
        peak = jnp.max(log_weight, axis=0, keepdims=True)
        weight = jnp.exp(log_weight - peak)
        total = jnp.sum(weight, axis=0, keepdims=True)
        weight_ref[c] = weight
        for b in range(per):
            stats_ref[c * per + b, 0:1] = peak[:, b * LANES : (b + 1) * LANES]
            stats_ref[c * per + b, 1:2] = total[:, b * LANES : (b + 1) * LANES]


def weights(earlier, later):
    count, points = later.shape[0], earlier.shape[0] * LANES
    per = 2 if count % 2 == 0 else 1
    return pl.pallas_call(
        weights_kernel,
        out_shape=(
            jax.ShapeDtypeStruct((count // per, points, per * LANES), jnp.float32),
            jax.ShapeDtypeStruct((count, 2, LANES), jnp.float32),
        ),
        in_specs=[pl.BlockSpec(memory_space=pltpu.VMEM)] * 2,
        out_specs=(pl.BlockSpec(memory_space=pltpu.VMEM),) * 2,
        cost_estimate=pl.CostEstimate(
            flops=2 * 256 * points * count * LANES,
            bytes_accessed=4 * points * count * LANES,
            transcendentals=points * count * LANES,
        ),
        name="weights",
    )(earlier, later)


def project(weight_ref, local_ref, joined_ref, values, out_ref):
    total = None
    per = weight_ref.shape[2] // LANES
    for c in range(weight_ref.shape[0]):
        blocks = range(c * per, (c + 1) * per)
        scale = jnp.concatenate([jnp.exp(local_ref[b, 0:1] - joined_ref[b, 0:1]) for b in blocks], axis=1)
        scaled = jnp.concatenate([values(b) / joined_ref[b, 1:2] for b in blocks], axis=1).astype(jnp.bfloat16)
        kernel = (weight_ref[c] * scale).astype(jnp.bfloat16)
        term = lax.dot_general(scaled, kernel, (((1,), (1,)), ((), ())), preferred_element_type=jnp.float32)
        total = term if total is None else total + term
    for b in range(out_ref.shape[0]):
        out_ref[b] = total[:, b * LANES : (b + 1) * LANES]


def first_kernel(weight_ref, local_ref, joined_ref, value_ref, out_ref):
    project(weight_ref, local_ref, joined_ref, lambda b: value_ref[b], out_ref)


def second_kernel(weight_ref, local_ref, joined_ref, sum_ref, payoff_ref, out_ref, value_ref):
    value_ref[...] = jnp.maximum(payoff_ref[0], sum_ref[0])
    project(weight_ref, local_ref, joined_ref, lambda b: jnp.maximum(payoff_ref[b], sum_ref[b]), out_ref)


def continuation(weight, local, joined, *values):
    points = weight.shape[1]
    swaps = values[0].shape[1]
    out = jax.ShapeDtypeStruct((points // LANES, swaps, LANES), jnp.float32)
    second = len(values) == 2
    outs = (out, jax.ShapeDtypeStruct((swaps, LANES), jnp.float32)) if second else out
    vmem = pl.BlockSpec(memory_space=pltpu.VMEM)
    return pl.pallas_call(
        second_kernel if second else first_kernel,
        out_shape=outs,
        in_specs=[vmem] * (3 + len(values)),
        out_specs=(vmem, vmem) if second else vmem,
        cost_estimate=pl.CostEstimate(
            flops=2 * swaps * weight.size, bytes_accessed=4 * weight.size, transcendentals=weight.size // points
        ),
        name="project",
    )(weight, local, joined, *values)


def per_device(states_now, states_next, states_last, payoff_now, payoff_next, payoff_last):
    row_size, col_size = lax.axis_size("row"), lax.axis_size("col")
    far = list(reversed([("row", 1)] + bits("col", 1, col_size)))
    near = bits("row", 1, row_size) + bits("col", 0, 2)
    wide = jnp.float32
    last = gathered(states_last[None], far)
    following = gathered(states_next[None], near)
    weight1, local1 = weights(following, last)
    joined1 = joined_stats(local1, far)
    last_value = gathered(payoff_last.astype(wide)[None], far)
    sum1 = summed(continuation(weight1, local1, joined1, last_value), near)

    now = gathered(states_now[None], far)
    weight2, local2 = weights(now, following)
    joined2 = joined_stats(local2, near)
    next_payoff = gathered(payoff_next.astype(wide)[None], near)
    sum2, value_next = continuation(weight2, local2, joined2, sum1, next_payoff)
    value_now = jnp.maximum(payoff_now.astype(wide), scattered(sum2, far)[0])
    return (value_next, value_now)


def solution(mesh):
    in_specs = (
        P(None, ("col", "row")),
        P(None, ("row", "col")),
        P(None, ("col", "row")),
        P(None, ("col", "row")),
        P(None, ("row", "col")),
        P(None, ("col", "row")),
    )
    out_specs = (P(None, ("row", "col")), P(None, ("col", "row")))
    return jax.shard_map(per_device, mesh=mesh, in_specs=in_specs, out_specs=out_specs, check_vma=False)
```

time: 199 us -> 74.6 us (0.37)
  blocking collectives: 154 us -> 0 us
  starting transfers between devices: 0.08 us -> 21.5 us
  between operations: 14.2 us -> 0.78 us
  other arithmetic: 3.48 us -> 16 us
  Pallas kernels: 0 us -> 11.8 us
  matrix products: 5.77 us -> 0 us
  waiting for transfers between devices: 19 us -> 22.7 us
    all_gather x7 -> x0, blocking collectives: 141 us -> none  [the longest x2 61.3 us: merged(): everything = jax.tree.map(lambda part: lax.all_gather(part, axis), array)]
    ppermute x0 -> x23, waiting for transfers between devices: none -> 22.7 us  [swapped(): return lax.ppermute(array, axis, pairs)]
    ppermute x0 -> x23, starting transfers between devices: none -> 21.5 us  [swapped(): return lax.ppermute(array, axis, pairs)]
    reduce_scatter x1 -> x0, waiting for transfers between devices: 19 us -> none  [per_device(): lax.psum_scatter(partial_value, 'row', scatter_dimension=1, tiled=True)]
    pallas_call x0 -> x4, Pallas kernels: none -> 11.8 us  [the longest x2 6.23 us: weights(): pl.pallas_call(weights_kernel, out_shape=(jax.ShapeDtypeStruct((count //...]
    concatenate x0 -> x18, other arithmetic: none -> 9.76 us  [the longest x13 8.52 us: gathered(): block = jnp.concatenate([block, swapped(block, link)], axis=0)]
    pmax x1 -> x0, blocking collectives: 7.11 us -> none  [stats_row(): global_peak = lax.pmax(col_peak, 'row')]
    psum x1 -> x0, blocking collectives: 5.88 us -> none  [stats_row(): global_sum = lax.psum(col_sum * jnp.exp(col_peak - global_peak), 'row')]
  transfers between devices with their start and end apart: 2 -> 23, of which waited for: 1 -> 9; matrix products, arithmetic and copies ran while one was open for 2% -> 17% of each run, Pallas kernels for 0% -> 12%
where the time goes in v1:
time: 74.6 us; the launch traced here: 73.8 us
  waiting for transfers between devices  22.7 us (30%)
  starting transfers between devices  21.5 us (29%)
  other arithmetic  16 us (21%)
  Pallas kernels  11.8 us (16%)
  local copies, waits for them, and re-layouts  0.97 us (1%)
  between operations  0.78 us (1%)
    ppermute x23, waiting for transfers between devices, swapped(): return lax.ppermute(array, axis, pairs)  22.7 us
    ppermute x23, starting transfers between devices, swapped(): return lax.ppermute(array, axis, pairs)  21.5 us
    concatenate x13, other arithmetic, gathered(): block = jnp.concatenate([block, swapped(block, link)], axis=0)  8.52 us
    pallas_call x2, Pallas kernels, weights(): pl.pallas_call(weights_kernel, out_shape=(jax.ShapeDtypeStruct((count //...  6.23 us
    pallas_call x2, Pallas kernels, continuation(): pl.pallas_call(second_kernel if second else first_kernel, out_shape=outs,...  5.56 us
    add x2, other arithmetic, summed(): array = array + flipped(swapped(array, link), level)  1.6 us
    add x3, other arithmetic, joined_stats(): stats[:, 1:] * jnp.exp(stats[:, :1] - peak)  1.59 us
  transfers between devices with their start and end apart: 23, of which 9 were waited for; matrix products, arithmetic and copies ran while one was open for 17% of the time, Pallas kernels for 12%

profile of v1, /device:TPU:0, one launch (start us, length us, event | category | flops | bytes accessed | tf_op | source)
XLA Modules:
  0.0 73.8 jit_solution(18146721036193853444)
XLA Ops:
  0.6 4.1 %collective-permute-start.7 = (f32[1,40,128]{2,1,0:T(8,128)}, f32[1,40,128]{2,1,0:T(8,128)S(1)}, u32[]{:S(2)}, u32[]{:S(2)}) collective-permute-start(f32[1,40,128]{2,1,0:T(8,128)} %bitcast.29), channel_id=1, source_target_pairs={{0,4},{1,5},{2,6},{3,7},{4,0},{5,1},{6,2},{7,3},{8,12},{9,13},{10,... | collective-permute-start | bytes 61448 | tf_op jit(solution)/shard_map/ppermute | solution.py:17
  4.8 1.5 %collective-permute-start.3 = (f32[1,40,128]{2,1,0:T(8,128)}, f32[1,40,128]{2,1,0:T(8,128)S(1)}, u32[]{:S(2)}, u32[]{:S(2)}) collective-permute-start(f32[1,40,128]{2,1,0:T(8,128)} %bitcast.39), channel_id=1, source_target_pairs={{0,16},{8,24},{16,0},{24,8},{1,17},{9,25},{17,1},{25,9},{2,18},{10... | collective-permute-start | bytes 61448 | tf_op jit(solution)/shard_map/ppermute | solution.py:17
  6.3 0.7 bitcast_convert_fusion.1
  7.3 2.6 %collective-permute-start = (f32[1,40,128]{2,1,0:T(8,128)}, f32[1,40,128]{2,1,0:T(8,128)S(1)}, u32[]{:S(2)}, u32[]{:S(2)}) collective-permute-start(f32[1,40,128]{2,1,0:T(8,128)} %bitcast.33), channel_id=1, source_target_pairs={{0,4},{1,5},{2,6},{3,7},{4,0},{5,1},{6,2},{7,3},{8,12},{9,13},{10,... | collective-permute-start | bytes 61448 | tf_op jit(solution)/shard_map/ppermute | solution.py:17
  9.9 0.7 bitcast_convert_fusion
  11.2 0.7 pad_maximum_fusion.12
  11.9 1.6 %collective-permute-start.8 = (f32[2,40,128]{2,1,0:T(8,128)S(1)}, f32[2,40,128]{2,1,0:T(8,128)S(1)}, u32[]{:S(2)}, u32[]{:S(2)}) collective-permute-start(f32[2,40,128]{2,1,0:T(8,128)S(1)} %pad_maximum_fusion.12), channel_id=1, source_target_pairs={{0,2},{1,3},{2,0},{3,1},{4,6},{5,7},{6,4},{7,5},{8,10},{9,11},{10,... | collective-permute-start | bytes 122888 | tf_op jit(solution)/shard_map/ppermute | solution.py:17
  13.5 0.7 pad_maximum_fusion.11
  14.2 1.5 %collective-permute-start.4 = (f32[2,40,128]{2,1,0:T(8,128)S(1)}, f32[2,40,128]{2,1,0:T(8,128)S(1)}, u32[]{:S(2)}, u32[]{:S(2)}) collective-permute-start(f32[2,40,128]{2,1,0:T(8,128)S(1)} %pad_maximum_fusion.11), channel_id=1, source_target_pairs={{0,1},{1,0},{2,3},{3,2},{4,5},{5,4},{6,7},{7,6},{8,9},{9,8},{10,11... | collective-permute-start | bytes 122888 | tf_op jit(solution)/shard_map/ppermute | solution.py:17
  15.7 0.7 pad_maximum_fusion.10
  16.9 1.6 %collective-permute-start.14 = (f32[2,64,128]{2,1,0:T(8,128)S(1)}, f32[2,64,128]{2,1,0:T(8,128)S(1)}, u32[]{:S(2)}, u32[]{:S(2)}) collective-permute-start(f32[2,64,128]{2,1,0:T(8,128)S(1)} %pad_maximum_fusion.8), channel_id=1, source_target_pairs={{0,2},{1,3},{2,0},{3,1},{4,6},{5,7},{6,4},{7,5},{8,10},{9,11},{10,... | collective-permute-start | bytes 196616 | tf_op jit(solution)/shard_map/ppermute | solution.py:17
  18.6 0.6 collective-permute-start.19
  19.2 0.7 pad_maximum_fusion.7
  19.9 0.5 collective-permute-done.1
  20.4 0.7 pad_maximum_fusion.5
  21.2 1.4 %pad_maximum_fusion.6.later_ref.earlier_ref = f32[4,40,128]{2,1,0:T(8,128)} fusion(f32[2,40,128]{2,1,0:T(8,128)S(1)} %collective-permute-done.4, f32[1,40,128]{2,1,0:T(8,128)S(1)} %collective-permute-done.3, f32[1,40,128]{2,1,0:T(8,128)} %bitcast.41), kind=kLoop, calls=%fused_computation.9 | loop fusion | flops 40960 | bytes 163840 | tf_op jit(solution)/shard_map/concatenate | solution.py:27
  22.6 1.4 %pad_maximum_fusion.2.later_ref = f32[8,40,128]{2,1,0:T(8,128)} fusion(f32[4,40,128]{2,1,0:T(8,128)S(1)} %collective-permute-done.9, f32[2,40,128]{2,1,0:T(8,128)S(1)} %collective-permute-done.8, f32[1,40,128]{2,1,0:T(8,128)S(1)} %collective-permute-done.7, f32[1,40,128]{2,1,0:T(8,128)} %bitcast.32), kind=kLoop, calls=%fused_computation.2 | loop fusion | flops 122880 | bytes 327680 | tf_op jit(solution)/shard_map/concatenate | solution.py:27
  24.0 3.1 %weights.3 = (f32[4,512,256]{2,1,0:T(8,128)}, f32[8,2,128]{2,1,0:T(2,128)}) custom-call(f32[4,40,128]{2,1,0:T(8,128)} %pad_maximum_fusion.6.later_ref.earlier_ref, f32[8,40,128]{2,1,0:T(8,128)} %pad_maximum_fusion.2.later_ref), custom_call_target="tpu_custom_call" | custom-call | flops 268435456 | bytes 2097152 | tf_op jit(solution)/shard_map/weights/pallas_call | solution.py:102
  27.0 0.5 collective-permute-start.10
  27.5 0.7 pad_maximum_fusion.1.earlier_ref
  28.2 3.2 %weights.2 = (f32[2,1024,256]{2,1,0:T(8,128)}, f32[4,2,128]{2,1,0:T(2,128)}) custom-call(f32[8,40,128]{2,1,0:T(8,128)} %pad_maximum_fusion.1.earlier_ref, f32[4,40,128]{2,1,0:T(8,128)} %pad_maximum_fusion.6.later_ref.earlier_ref), custom_call_target="tpu_custom_call" | custom-call | flops 268435456 | bytes 2097152 | tf_op jit(solution)/shard_map/weights/pallas_call | solution.py:102
  31.4 0.9 %collective-permute-start.5 = (f32[4,2,128]{2,1,0:T(2,128)}, f32[4,2,128]{2,1,0:T(2,128)S(1)}, u32[]{:S(2)}, u32[]{:S(2)}) collective-permute-start(f32[4,2,128]{2,1,0:T(2,128)} %get-tuple-element.9.local_ref), channel_id=1, source_target_pairs={{0,1},{1,0},{2,3},{3,2},{4,5},{5,4},{6,7},{7,6},{8,9},{9,8},{10,11... | collective-permute-start | bytes 12296 | tf_op jit(solution)/shard_map/ppermute | solution.py:17
  32.4 0.8 %fusion.4 = (f32[8,1,128]{2,1,0:T(1,128)S(1)}, f32[8,1,128]{2,1,0:T(1,128)S(1)}) fusion(f32[8,2,128]{2,1,0:T(2,128)S(1)} %bitcast.44, f32[8,2,128]{2,1,0:T(2,128)} %get-tuple-element.11.local_ref), kind=kLoop, calls=%fused_computation.30 | loop fusion | flops 6144 | bytes 24576 | tf_op jit(solution)/shard_map/add | solution.py:55
  33.2 0.5 collective-permute-start.11
  33.8 1.4 %collective-permute-done.5 = f32[4,2,128]{2,1,0:T(2,128)S(1)} collective-permute-done((f32[4,2,128]{2,1,0:T(2,128)}, f32[4,2,128]{2,1,0:T(2,128)S(1)}, u32[]{:S(2)}, u32[]{:S(2)}) %collective-permute-start.5) | collective-permute-done | bytes 4128 | tf_op jit(solution)/shard_map/ppermute | solution.py:17
  35.2 1.7 %collective-permute-done.11 = f32[8,2,128]{2,1,0:T(2,128)S(1)} collective-permute-done((f32[8,2,128]{2,1,0:T(2,128)S(1)}, f32[8,2,128]{2,1,0:T(2,128)S(1)}, u32[]{:S(2)}, u32[]{:S(2)}) %collective-permute-start.11) | collective-permute-done | bytes 8224 | tf_op jit(solution)/shard_map/ppermute | solution.py:17
  37.3 0.8 %fusion.6 = (f32[4,1,128]{2,1,0:T(1,128)S(1)}, f32[4,1,128]{2,1,0:T(1,128)S(1)}) fusion(f32[4,2,128]{2,1,0:T(2,128)S(1)} %bitcast.45, f32[4,2,128]{2,1,0:T(2,128)} %get-tuple-element.9.local_ref), kind=kLoop, calls=%fused_computation.39 | loop fusion | flops 3072 | bytes 12288 | tf_op jit(solution)/shard_map/add | solution.py:55
  38.1 3.4 %collective-permute-done.12 = f32[8,2,128]{2,1,0:T(2,128)S(1)} collective-permute-done((f32[8,2,128]{2,1,0:T(2,128)S(1)}, f32[8,2,128]{2,1,0:T(2,128)S(1)}, u32[]{:S(2)}, u32[]{:S(2)}) %collective-permute-start.12) | collective-permute-done | bytes 8224 | tf_op jit(solution)/shard_map/ppermute | solution.py:17
  41.6 0.6 pad_maximum_fusion.15.joined_ref
  42.2 0.7 pad_maximum_fusion.value_ref
  42.9 2.7 %project.2 = f32[4,64,128]{2,1,0:T(8,128)} custom-call(f32[4,512,256]{2,1,0:T(8,128)} %get-tuple-element.10.weight_ref, f32[8,2,128]{2,1,0:T(2,128)} %get-tuple-element.11.local_ref, f32[8,2,128]{2,1,0:T(2,128)} %pad_maximum_fusion.15.joined_ref, f32[8,64,128]{2,1,0:T(8,128)} %pad_maximum_fusion.value_ref), custom_call_target="tpu_custom_call" | custom-call | flops 67108864 | bytes 2097152 | tf_op jit(solution)/shard_map/project/pallas_call | solution.py:149
  45.6 1.5 %collective-permute-start.16 = (f32[4,64,128]{2,1,0:T(8,128)}, f32[4,64,128]{2,1,0:T(8,128)S(1)}, u32[]{:S(2)}, u32[]{:S(2)}) collective-permute-start(f32[4,64,128]{2,1,0:T(8,128)} %project.2), channel_id=1, source_target_pairs={{0,16},{8,24},{16,0},{24,8},{1,17},{9,25},{17,1},{25,9},{2,18},{10... | collective-permute-start | bytes 393224 | tf_op jit(solution)/shard_map/ppermute | solution.py:17
  47.2 0.6 collective-permute-start.6
  47.7 0.7 pad_maximum_fusion.4.payoff_ref
  48.4 2.5 %collective-permute-done.6 = f32[4,2,128]{2,1,0:T(2,128)S(1)} collective-permute-done((f32[4,2,128]{2,1,0:T(2,128)S(1)}, f32[4,2,128]{2,1,0:T(2,128)S(1)}, u32[]{:S(2)}, u32[]{:S(2)}) %collective-permute-start.6) | collective-permute-done | bytes 4128 | tf_op jit(solution)/shard_map/ppermute | solution.py:17
  50.9 0.9 %bitcast_add_fusion.1 = f32[4,64,128]{2,1,0:T(8,128)S(1)} fusion(f32[4,64,128]{2,1,0:T(8,128)} %project.2, f32[2,2,1,64,128]{4,3,1,0,2:T(8,128)S(1)} %rev.33), kind=kLoop, calls=%fused_computation.6 | loop fusion | flops 32768 | bytes 393216 | tf_op jit(solution)/shard_map/add | solution.py:40
  51.8 1.1 %collective-permute-start.17 = (f32[4,64,128]{2,1,0:T(8,128)S(1)}, f32[4,64,128]{2,1,0:T(8,128)S(1)}, u32[]{:S(2)}, u32[]{:S(2)}) collective-permute-start(f32[4,64,128]{2,1,0:T(8,128)S(1)} %bitcast_add_fusion.1), channel_id=1, source_target_pairs={{0,1},{1,0},{2,3},{3,2},{4,5},{5,4},{6,7},{7,6},{8,9},{9,8},{10,11... | collective-permute-start | bytes 393224 | tf_op jit(solution)/shard_map/ppermute | solution.py:17
  53.0 0.6 pad_maximum_fusion.17.joined_ref
  53.6 3.3 %collective-permute-done.17 = f32[4,64,128]{2,1,0:T(8,128)S(1)} collective-permute-done((f32[4,64,128]{2,1,0:T(8,128)S(1)}, f32[4,64,128]{2,1,0:T(8,128)S(1)}, u32[]{:S(2)}, u32[]{:S(2)}) %collective-permute-start.17) | collective-permute-done | bytes 131104 | tf_op jit(solution)/shard_map/ppermute | solution.py:17
  56.9 0.7 bitcast_add_fusion.sum_ref
  57.5 2.8 %project.3 = (f32[8,64,128]{2,1,0:T(8,128)}, f32[64,128]{1,0:T(8,128)}) custom-call(f32[2,1024,256]{2,1,0:T(8,128)} %get-tuple-element.8.weight_ref, f32[4,2,128]{2,1,0:T(2,128)} %get-tuple-element.9.local_ref, f32[4,2,128]{2,1,0:T(2,128)} %pad_maximum_fusion.17.joined_ref, f32[4,64,128]{2,1,0:T(8,128)} %bitcast_add_fusion.sum_ref, ...), custom_call_target="tpu_custom_call" | custom-call | flops 67108864 | bytes 2097152 | tf_op jit(solution)/shard_map/project/pallas_call | solution.py:149
  60.4 0.9 %slice.82 = f32[4,64,128]{2,1,0:T(8,128)S(1)} slice(f32[8,64,128]{2,1,0:T(8,128)} %get-tuple-element.13), slice={[4:8], [0:64], [0:128]} | slice | bytes 262144 | tf_op jit(solution)/shard_map/slice | solution.py:47
  61.4 1.3 %collective-permute-done.20 = f32[4,64,128]{2,1,0:T(8,128)S(1)} collective-permute-done((f32[4,64,128]{2,1,0:T(8,128)S(1)}, f32[4,64,128]{2,1,0:T(8,128)S(1)}, u32[]{:S(2)}, u32[]{:S(2)}) %collective-permute-start.20) | collective-permute-done | bytes 131104 | tf_op jit(solution)/shard_map/ppermute | solution.py:17
  62.7 0.9 %slice_add_fusion = f32[4,64,128]{2,1,0:T(8,128)S(1)} fusion(f32[4,64,128]{2,1,0:T(8,128)S(1)} %collective-permute-done.20, f32[8,64,128]{2,1,0:T(8,128)} %get-tuple-element.13), kind=kLoop, calls=%fused_computation.7 | loop fusion | flops 32768 | bytes 393216 | tf_op jit(solution)/shard_map/add | solution.py:47
  63.7 0.5 collective-permute-start.21
  64.2 3.8 %collective-permute-done.21 = f32[2,64,128]{2,1,0:T(8,128)S(1)} collective-permute-done((f32[2,64,128]{2,1,0:T(8,128)S(1)}, f32[2,64,128]{2,1,0:T(8,128)S(1)}, u32[]{:S(2)}, u32[]{:S(2)}) %collective-permute-start.21) | collective-permute-done | bytes 65568 | tf_op jit(solution)/shard_map/ppermute | solution.py:17
  68.4 4.7 %collective-permute-done.22 = f32[1,64,128]{2,1,0:T(8,128)S(1)} collective-permute-done((f32[1,64,128]{2,1,0:T(8,128)S(1)}, f32[1,64,128]{2,1,0:T(8,128)S(1)}, u32[]{:S(2)}, u32[]{:S(2)}) %collective-permute-start.22) | collective-permute-done | bytes 32800 | tf_op jit(solution)/shard_map/ppermute | solution.py:17
  73.1 0.6 fusion.1
  (46 shorter events, 2.5 us)
Async XLA Ops:
  0.6 26.9 %copy-start = (f32[40,128]{1,0:T(8,128)S(1)}, f32[40,128]{1,0:T(8,128)}, u32[]{:S(2)}) copy-start(f32[40,128]{1,0:T(8,128)} %param.6) | copy-start | bytes 61444
  0.6 10.5 %collective-permute-start.7 = (f32[1,40,128]{2,1,0:T(8,128)}, f32[1,40,128]{2,1,0:T(8,128)S(1)}, u32[]{:S(2)}, u32[]{:S(2)}) collective-permute-start(f32[1,40,128]{2,1,0:T(8,128)} %bitcast.29), channel_id=1, source_target_pairs={{0,4},{1,5},{2,6},{3,7},{4,0},{5,1},{6,2},{7,3},{8,12},{9,13},{10,... | collective-permute-start | bytes 61448 | tf_op jit(solution)/shard_map/ppermute | solution.py:17
  4.8 8.7 %collective-permute-start.3 = (f32[1,40,128]{2,1,0:T(8,128)}, f32[1,40,128]{2,1,0:T(8,128)S(1)}, u32[]{:S(2)}, u32[]{:S(2)}) collective-permute-start(f32[1,40,128]{2,1,0:T(8,128)} %bitcast.39), channel_id=1, source_target_pairs={{0,16},{8,24},{16,0},{24,8},{1,17},{9,25},{17,1},{25,9},{2,18},{10... | collective-permute-start | bytes 61448 | tf_op jit(solution)/shard_map/ppermute | solution.py:17
  7.0 9.9 %collective-permute-start.13 = (f32[1,64,128]{2,1,0:T(8,128)S(1)}, f32[1,64,128]{2,1,0:T(8,128)S(1)}, u32[]{:S(2)}, u32[]{:S(2)}) collective-permute-start(f32[1,64,128]{2,1,0:T(8,128)S(1)} %bitcast_convert_fusion.1), channel_id=1, source_target_pairs={{0,4},{1,5},{2,6},{3,7},{4,0},{5,1},{6,2},{7,3},{8,12},{9,13},{10,... | collective-permute-start | bytes 98312 | tf_op jit(solution)/shard_map/ppermute | solution.py:17
  7.3 8.4 %collective-permute-start = (f32[1,40,128]{2,1,0:T(8,128)}, f32[1,40,128]{2,1,0:T(8,128)S(1)}, u32[]{:S(2)}, u32[]{:S(2)}) collective-permute-start(f32[1,40,128]{2,1,0:T(8,128)} %bitcast.33), channel_id=1, source_target_pairs={{0,4},{1,5},{2,6},{3,7},{4,0},{5,1},{6,2},{7,3},{8,12},{9,13},{10,... | collective-permute-start | bytes 61448 | tf_op jit(solution)/shard_map/ppermute | solution.py:17
  10.7 7.9 %collective-permute-start.18 = (f32[1,64,128]{2,1,0:T(8,128)S(1)}, f32[1,64,128]{2,1,0:T(8,128)S(1)}, u32[]{:S(2)}, u32[]{:S(2)}) collective-permute-start(f32[1,64,128]{2,1,0:T(8,128)S(1)} %bitcast_convert_fusion), channel_id=1, source_target_pairs={{0,16},{8,24},{16,0},{24,8},{1,17},{9,25},{17,1},{25,9},{2,18},{10... | collective-permute-start | bytes 98312 | tf_op jit(solution)/shard_map/ppermute | solution.py:17
  11.9 7.3 %collective-permute-start.8 = (f32[2,40,128]{2,1,0:T(8,128)S(1)}, f32[2,40,128]{2,1,0:T(8,128)S(1)}, u32[]{:S(2)}, u32[]{:S(2)}) collective-permute-start(f32[2,40,128]{2,1,0:T(8,128)S(1)} %pad_maximum_fusion.12), channel_id=1, source_target_pairs={{0,2},{1,3},{2,0},{3,1},{4,6},{5,7},{6,4},{7,5},{8,10},{9,11},{10,... | collective-permute-start | bytes 122888 | tf_op jit(solution)/shard_map/ppermute | solution.py:17
  14.2 7.0 %collective-permute-start.4 = (f32[2,40,128]{2,1,0:T(8,128)S(1)}, f32[2,40,128]{2,1,0:T(8,128)S(1)}, u32[]{:S(2)}, u32[]{:S(2)}) collective-permute-start(f32[2,40,128]{2,1,0:T(8,128)S(1)} %pad_maximum_fusion.11), channel_id=1, source_target_pairs={{0,1},{1,0},{2,3},{3,2},{4,5},{5,4},{6,7},{7,6},{8,9},{9,8},{10,11... | collective-permute-start | bytes 122888 | tf_op jit(solution)/shard_map/ppermute | solution.py:17
  16.4 4.0 %collective-permute-start.1 = (f32[2,40,128]{2,1,0:T(8,128)S(1)}, f32[2,40,128]{2,1,0:T(8,128)S(1)}, u32[]{:S(2)}, u32[]{:S(2)}) collective-permute-start(f32[2,40,128]{2,1,0:T(8,128)S(1)} %pad_maximum_fusion.10), channel_id=1, source_target_pairs={{0,2},{1,3},{2,0},{3,1},{4,6},{5,7},{6,4},{7,5},{8,10},{9,11},{10,... | collective-permute-start | bytes 122888 | tf_op jit(solution)/shard_map/ppermute | solution.py:17
  16.9 16.8 %collective-permute-start.14 = (f32[2,64,128]{2,1,0:T(8,128)S(1)}, f32[2,64,128]{2,1,0:T(8,128)S(1)}, u32[]{:S(2)}, u32[]{:S(2)}) collective-permute-start(f32[2,64,128]{2,1,0:T(8,128)S(1)} %pad_maximum_fusion.8), channel_id=1, source_target_pairs={{0,2},{1,3},{2,0},{3,1},{4,6},{5,7},{6,4},{7,5},{8,10},{9,11},{10,... | collective-permute-start | bytes 196616 | tf_op jit(solution)/shard_map/ppermute | solution.py:17
  18.6 29.2 %collective-permute-start.19 = (f32[2,64,128]{2,1,0:T(8,128)S(1)}, f32[2,64,128]{2,1,0:T(8,128)S(1)}, u32[]{:S(2)}, u32[]{:S(2)}) collective-permute-start(f32[2,64,128]{2,1,0:T(8,128)S(1)} %pad_maximum_fusion.9), channel_id=1, source_target_pairs={{0,1},{1,0},{2,3},{3,2},{4,5},{5,4},{6,7},{7,6},{8,9},{9,8},{10,11... | collective-permute-start | bytes 196616 | tf_op jit(solution)/shard_map/ppermute | solution.py:17
  19.9 2.7 %collective-permute-start.9 = (f32[4,40,128]{2,1,0:T(8,128)S(1)}, f32[4,40,128]{2,1,0:T(8,128)S(1)}, u32[]{:S(2)}, u32[]{:S(2)}) collective-permute-start(f32[4,40,128]{2,1,0:T(8,128)S(1)} %pad_maximum_fusion.7), channel_id=1, source_target_pairs={{0,8},{8,0},{16,24},{24,16},{1,9},{9,1},{17,25},{25,17},{2,10},{10... | collective-permute-start | bytes 245768 | tf_op jit(solution)/shard_map/ppermute | solution.py:17
  21.2 6.4 %collective-permute-start.2 = (f32[4,40,128]{2,1,0:T(8,128)S(1)}, f32[4,40,128]{2,1,0:T(8,128)S(1)}, u32[]{:S(2)}, u32[]{:S(2)}) collective-permute-start(f32[4,40,128]{2,1,0:T(8,128)S(1)} %pad_maximum_fusion.5), channel_id=1, source_target_pairs={{0,8},{8,0},{16,24},{24,16},{1,9},{9,1},{17,25},{25,17},{2,10},{10... | collective-permute-start | bytes 245768 | tf_op jit(solution)/shard_map/ppermute | solution.py:17
  27.0 5.3 %collective-permute-start.10 = (f32[8,2,128]{2,1,0:T(2,128)}, f32[8,2,128]{2,1,0:T(2,128)S(1)}, u32[]{:S(2)}, u32[]{:S(2)}) collective-permute-start(f32[8,2,128]{2,1,0:T(2,128)} %get-tuple-element.11.local_ref), channel_id=1, source_target_pairs={{0,8},{8,0},{16,24},{24,16},{1,9},{9,1},{17,25},{25,17},{2,10},{10... | collective-permute-start | bytes 24584 | tf_op jit(solution)/shard_map/ppermute | solution.py:17
  31.4 3.8 %collective-permute-start.5 = (f32[4,2,128]{2,1,0:T(2,128)}, f32[4,2,128]{2,1,0:T(2,128)S(1)}, u32[]{:S(2)}, u32[]{:S(2)}) collective-permute-start(f32[4,2,128]{2,1,0:T(2,128)} %get-tuple-element.9.local_ref), channel_id=1, source_target_pairs={{0,1},{1,0},{2,3},{3,2},{4,5},{5,4},{6,7},{7,6},{8,9},{9,8},{10,11... | collective-permute-start | bytes 12296 | tf_op jit(solution)/shard_map/ppermute | solution.py:17
  33.2 3.7 %collective-permute-start.11 = (f32[8,2,128]{2,1,0:T(2,128)S(1)}, f32[8,2,128]{2,1,0:T(2,128)S(1)}, u32[]{:S(2)}, u32[]{:S(2)}) collective-permute-start(f32[8,2,128]{2,1,0:T(2,128)S(1)} %pad_maximum_fusion.13), channel_id=1, source_target_pairs={{0,2},{1,3},{2,0},{3,1},{4,6},{5,7},{6,4},{7,5},{8,10},{9,11},{10,... | collective-permute-start | bytes 24584 | tf_op jit(solution)/shard_map/ppermute | solution.py:17
  33.7 8.5 %collective-permute-start.15 = (f32[4,64,128]{2,1,0:T(8,128)S(1)}, f32[4,64,128]{2,1,0:T(8,128)S(1)}, u32[]{:S(2)}, u32[]{:S(2)}) collective-permute-start(f32[4,64,128]{2,1,0:T(8,128)S(1)} %pad_maximum_fusion.3), channel_id=1, source_target_pairs={{0,8},{8,0},{16,24},{24,16},{1,9},{9,1},{17,25},{25,17},{2,10},{10... | collective-permute-start | bytes 393224 | tf_op jit(solution)/shard_map/ppermute | solution.py:17
  36.9 4.6 %collective-permute-start.12 = (f32[8,2,128]{2,1,0:T(2,128)S(1)}, f32[8,2,128]{2,1,0:T(2,128)S(1)}, u32[]{:S(2)}, u32[]{:S(2)}) collective-permute-start(f32[8,2,128]{2,1,0:T(2,128)S(1)} %pad_maximum_fusion.14), channel_id=1, source_target_pairs={{0,4},{1,5},{2,6},{3,7},{4,0},{5,1},{6,2},{7,3},{8,12},{9,13},{10,... | collective-permute-start | bytes 24584 | tf_op jit(solution)/shard_map/ppermute | solution.py:17
  45.6 5.2 %collective-permute-start.16 = (f32[4,64,128]{2,1,0:T(8,128)}, f32[4,64,128]{2,1,0:T(8,128)S(1)}, u32[]{:S(2)}, u32[]{:S(2)}) collective-permute-start(f32[4,64,128]{2,1,0:T(8,128)} %project.2), channel_id=1, source_target_pairs={{0,16},{8,24},{16,0},{24,8},{1,17},{9,25},{17,1},{25,9},{2,18},{10... | collective-permute-start | bytes 393224 | tf_op jit(solution)/shard_map/ppermute | solution.py:17
  47.2 3.7 %collective-permute-start.6 = (f32[4,2,128]{2,1,0:T(2,128)S(1)}, f32[4,2,128]{2,1,0:T(2,128)S(1)}, u32[]{:S(2)}, u32[]{:S(2)}) collective-permute-start(f32[4,2,128]{2,1,0:T(2,128)S(1)} %pad_maximum_fusion.16), channel_id=1, source_target_pairs={{0,16},{8,24},{16,0},{24,8},{1,17},{9,25},{17,1},{25,9},{2,18},{10... | collective-permute-start | bytes 12296 | tf_op jit(solution)/shard_map/ppermute | solution.py:17
  51.8 21.3 %copy-start.1 = (bf16[64,128]{1,0:T(8,128)(2,1)S(1)}, bf16[64,128]{1,0:T(8,128)(2,1)}, u32[]{:S(2)}) copy-start(bf16[64,128]{1,0:T(8,128)(2,1)} %param.9) | copy-start | bytes 49156
  51.8 5.0 %collective-permute-start.17 = (f32[4,64,128]{2,1,0:T(8,128)S(1)}, f32[4,64,128]{2,1,0:T(8,128)S(1)}, u32[]{:S(2)}, u32[]{:S(2)}) collective-permute-start(f32[4,64,128]{2,1,0:T(8,128)S(1)} %bitcast_add_fusion.1), channel_id=1, source_target_pairs={{0,1},{1,0},{2,3},{3,2},{4,5},{5,4},{6,7},{7,6},{8,9},{9,8},{10,11... | collective-permute-start | bytes 393224 | tf_op jit(solution)/shard_map/ppermute | solution.py:17
  61.3 1.4 %collective-permute-start.20 = (f32[4,64,128]{2,1,0:T(8,128)S(1)}, f32[4,64,128]{2,1,0:T(8,128)S(1)}, u32[]{:S(2)}, u32[]{:S(2)}) collective-permute-start(f32[4,64,128]{2,1,0:T(8,128)S(1)} %slice.82), channel_id=1, source_target_pairs={{0,8},{8,0},{16,24},{24,16},{1,9},{9,1},{17,25},{25,17},{2,10},{10... | collective-permute-start | bytes 393224 | tf_op jit(solution)/shard_map/ppermute | solution.py:17
  63.7 4.3 %collective-permute-start.21 = (f32[2,64,128]{2,1,0:T(8,128)S(1)}, f32[2,64,128]{2,1,0:T(8,128)S(1)}, u32[]{:S(2)}, u32[]{:S(2)}) collective-permute-start(f32[2,64,128]{2,1,0:T(8,128)S(1)} %slice.98), channel_id=1, source_target_pairs={{0,2},{1,3},{2,0},{3,1},{4,6},{5,7},{6,4},{7,5},{8,10},{9,11},{10,... | collective-permute-start | bytes 196616 | tf_op jit(solution)/shard_map/ppermute | solution.py:17
  68.0 5.1 %collective-permute-start.22 = (f32[1,64,128]{2,1,0:T(8,128)S(1)}, f32[1,64,128]{2,1,0:T(8,128)S(1)}, u32[]{:S(2)}, u32[]{:S(2)}) collective-permute-start(f32[1,64,128]{2,1,0:T(8,128)S(1)} %slice.100), channel_id=1, source_target_pairs={{0,4},{1,5},{2,6},{3,7},{4,0},{5,1},{6,2},{7,3},{8,12},{9,13},{10,... | collective-permute-start | bytes 98312 | tf_op jit(solution)/shard_map/ppermute | solution.py:17
